TPU v7x, 128 devices: a whole 4x4x4 slice. The times are simulated.
128 devices in a mesh: region: 128 (over x, y, z, core).
Axes of the slice: x: 4, y: 4, z: 4, core: 2. Of those that a mesh axis runs over, the one named last changes fastest.
Arguments:
- node_feat: bfloat16 [65536, 512], P('region'), may hold values from -6 to 6
- edge_feat: bfloat16 [524288, 512], P('region'), may hold values from -6 to 6
- sender: int32 [524288], P('region'), may hold values from 0 to 2815, as said below
- receiver: int32 [524288], P('region'), may hold values from 0 to 512, as said below
- send_list: int32 [128, 8, 32], P('region'), may hold values from 16 to 511
- edge_w1: bfloat16 [1536, 512], replicated, may hold values from -0.15625 to 0.15625
- edge_b1: float32 [512], replicated, may hold values from -4 to 4
- edge_w2: bfloat16 [512, 512], replicated, may hold values from -0.25 to 0.25
- edge_b2: float32 [512], replicated, may hold values from -4 to 4
- edge_gain: float32 [512], replicated, may hold values from 0.5 to 1.5
- edge_shift: float32 [512], replicated, may hold values from -4 to 4
- node_w1: bfloat16 [1024, 512], replicated, may hold values from -0.1875 to 0.1875
- node_b1: float32 [512], replicated, may hold values from -4 to 4
- node_w2: bfloat16 [512, 512], replicated, may hold values from -0.25 to 0.25
- node_b2: float32 [512], replicated, may hold values from -4 to 4
- node_gain: float32 [512], replicated, may hold values from 0.5 to 1.5
- node_shift: float32 [512], replicated, may hold values from -4 to 4
Outputs:
- edge_out: bfloat16 [524288, 512], P('region')
- node_out: bfloat16 [65536, 512], P('region')
Inputs may be any that keep to these rules, and one draw needn't show every extreme that they name: `sender`: a row of the region's table as built in the first step; every region has slots pointing at row 0 and at the last row. `receiver`: non-decreasing within each region's 4096 slots; the value 512 marks an empty slot, and empty slots stand after the used ones; some region uses all its slots. `send_list`: entry [s, j, k] is a local index on region s of a node that s sends to its j-th neighbour.
All inputs are finite; a program needn't handle non-finite values.
Results may differ from a plain program's by a relative error of at most 0.0043.
Values may be sent and summed in bfloat16 or wider, within the bound.
No kernel may reach another device: no remote copies, remote signals or barrier semaphores. Data moves between devices by JAX's collectives and lax.ppermute only.
A program may use at most 128 MiB of HBM per device.

v0:
```python
import jax
import jax.numpy as jnp
from jax import lax
from jax.experimental import pallas as pl
from jax.experimental.pallas import tpu as pltpu
from jax.sharding import PartitionSpec as P

COARSE_DEV = 16
BLOCK = 512
WINDOW = 128
HALF = BLOCK // 2
CHUNK = 64
OWN, OTHER, UP, DOWN, NEXT, SWAP, ROWS = 512, 1536, 2560, 2656, 2752, 2848, 2944
PHASES = ((2, 1, 0), (0, 2, 1))


def coords_of(region):
    return [region >> 5 & 3, region >> 3 & 3, region >> 1 & 3, region & 1]


def region_of(x, y, z, core):
    return ((x * 4 + y) * 4 + z) * 2 + core


def ring_route(phase, step):
    route = []
    for region in range(128):
        place = coords_of(region)
        dim = PHASES[place[3]][phase]
        place[dim] = (place[dim] + step) % 4
        route.append((region, region_of(*place)))
    return route


def linear_route(step):
    return [(i, (i + step) % 128) for i in range(128)]


def ring_phase(held, phase):
    parts = [held]
    parts += [lax.ppermute(held, "region", ring_route(phase, k)) for k in (1, 2, 3)]
    return jnp.concatenate(parts, axis=0)


def shifted(blocks, step):
    return lax.ppermute(jnp.concatenate(blocks, 0), "region", linear_route(step))


def coarse_places(index):
    me = lax.axis_index("region")
    mine = coords_of(me)
    row = index & 15
    theirs = coords_of(index >> 4)
    rel = [(mine[d] - theirs[d]) & 3 for d in range(3)]
    order = [(rel[c] * 16 + rel[b] * 4 + rel[a]) for a, b, c in PHASES]
    block = jnp.where(theirs[3] == 0, order[0], order[1])
    return jnp.where(theirs[3] == mine[3], 0, 1024) + block * 16 + row


def normed(y, gain_ref, shift_ref):
    mean = jnp.mean(y, axis=-1, keepdims=True)
    d = y - mean
    var = jnp.mean(d * d, axis=-1, keepdims=True)
    return d * lax.rsqrt(var + 1e-05) * gain_ref[...] + shift_ref[...]


def half_silu(u):
    return (u + u * jnp.tanh(u)).astype(jnp.bfloat16)


def dot(a, b):
    return jnp.dot(a, b, preferred_element_type=jnp.float32)


def window_hits(base, recv_row):
    ids = base + lax.broadcasted_iota(jnp.int32, (WINDOW, BLOCK), 0)
    return jnp.where(ids == recv_row, 1.0, 0.0).astype(jnp.bfloat16)


def project(src, lo, count, at, w1, ts):
    for r in range(0, count, 256):
        n = min(256, count - r)
        res = 0.5 * dot(src[lo + r : lo + r + n, :], w1[512:1024, :])
        for j in range(4):
            ts[pl.ds((at + r) * 4 + j, n, stride=4), :] = res[:, j * 128 : j * 128 + 128]


def first_kernel(
    node, w1, nw1, edge, nb1, recv_rows,
    node_v, w1_v, edge_v, high, low_bits, ts, node_part, bounds,
    nw_top, sems,
):
    moves = [(node, node_v), (w1, w1_v), (nw1.at[0:512, :], nw_top), (edge, edge_v)]
    copies = [pltpu.make_async_copy(a, b, sems.at[i]) for i, (a, b) in enumerate(moves)]
    for copy in copies:
        copy.start()
    recv = recv_rows[:, 0, :]
    used = jnp.where(recv < 512, 1, 0)
    bounds[16] = jnp.sum(used)
    for b in range(4096 // BLOCK):
        low = jnp.min(recv[b : b + 1, :]) >> 3 << 3
        bounds[b] = low
        bounds[8 + b] = (jnp.max(recv[b : b + 1, :]) - low) // WINDOW + 1
    copies[0].wait()
    copies[1].wait()
    tr = 0.5 * dot(node_v[...], w1_v[1024:1536, :])
    top = tr.astype(jnp.bfloat16)
    high[0:512, :] = top
    low_bits[0:512, :] = (tr - top.astype(jnp.float32)).astype(jnp.bfloat16)
    pad = jnp.zeros((high.shape[0] - 512, 512), jnp.bfloat16)
    high[512:, :] = pad
    low_bits[512:, :] = pad
    project(node_v, 0, 512, 0, w1_v, ts)
    copies[2].wait()
    node_part[...] = dot(node_v[...], nw_top[...]) + nb1[...]
    copies[3].wait()


def early_kernel(bounds, recv_rows, edge, w1, b1, high, low_bits, part):
    def pair(p, carry):
        spreads = []
        for i in range(2):
            b = p * 2 + i
            span = pl.ds(pl.multiple_of(b * BLOCK, BLOCK), BLOCK)

            def spread(k, b=b):
                base = pl.multiple_of(bounds[b] + k * WINDOW, 8)
                hits = window_hits(base, recv_rows[b])
                rows = jnp.concatenate([high[pl.ds(base, WINDOW), :], low_bits[pl.ds(base, WINDOW), :]], axis=0)
                return lax.dot_general(
                    jnp.concatenate([hits, hits], axis=0), rows,
                    (((0,), (0,)), ((), ())), preferred_element_type=jnp.float32,
                )

            part[span, :] = 0.5 * (dot(edge[span, :], w1[0:512, :]) + b1[...]) + spread(0)
            spreads.append((b, span, spread))

        for b, span, spread in spreads:

            def more(k, c, span=span, spread=spread):
                part[span, :] += spread(k)
                return c

            lax.fori_loop(1, bounds[8 + b], more, 0)
        return carry

    lax.fori_loop(0, 4096 // BLOCK // 2, pair, 0)


def table_kernel(own, up, down, beside, w1, old_ts, ts):
    del old_ts
    project(own, 0, 1024, OWN, w1, ts)
    project(up, 0, 96, UP, w1, ts)
    project(down, 0, 96, DOWN, w1, ts)
    project(beside, 0, 96, NEXT, w1, ts)


def layer_kernel(
    send_ref, bounds,
    recv_rows, part, edge, node, swapped, old_ts, w1, w2, b2, gain, shift,
    node_part, nw1, nw2, nb2, ngain, nshift,
    edge_out, node_out, ts,
    g0, g1, hid0, hid1, y1, acc, outs, out_sems,
):
    blocks = 4096 // BLOCK
    live = bounds[16]
    del old_ts

    def span(b):
        return pl.ds(pl.multiple_of(b * BLOCK, BLOCK), BLOCK)

    def copy_out(b):
        return pltpu.make_async_copy(outs.at[span(b), :], edge_out.at[span(b), :], out_sems.at[b])

    def rows_at(lo):
        return pl.ds(pl.multiple_of(lo, CHUNK), CHUNK)

    project(swapped, 0, 1024, OTHER, w1, ts)
    project(swapped, 1024, 96, SWAP, w1, ts)
    acc[...] = jnp.zeros_like(acc)
    y1[...] = jnp.zeros_like(y1)

    def fetch16(i, carry):
        for e in range(16):
            for g, at in ((g0, 0), (g1, HALF)):
                s = pl.multiple_of(send_ref[at + i * 16 + e], 4)
                g[pl.ds(pl.multiple_of(i * 64 + e * 4, 4), 4), :] = ts[pl.ds(s, 4), :]
        return carry

    lax.fori_loop(0, HALF // 16, fetch16, 0)
    pieces = HALF // CHUNK

    def silu_piece(c, first, g, hid):
        lo = c * CHUNK
        for j in range(4):
            cols = slice(j * 128, j * 128 + 128)
            u = part[rows_at(first + lo), cols] + g[pl.ds(lo * 4 + j, CHUNK, stride=4), :]
            hid[lo : lo + CHUNK, cols] = half_silu(u)

    def norm_piece(c, first, y):
        lo = c * CHUNK
        update = normed(y[lo : lo + CHUNK, :] + b2[...], gain, shift)
        rows = rows_at(first + lo)
        outs[rows, :] = (edge[rows, :].astype(jnp.float32) + update).astype(jnp.bfloat16)

    def fetch_piece(c, source, g):
        for e in range(c * CHUNK, (c + 1) * CHUNK):
            s = pl.multiple_of(send_ref[source + e], 4)
            g[e * 4 : e * 4 + 4, :] = ts[pl.ds(s, 4), :]

    def finish(b):
        first = b * BLOCK

        @pl.when(first + BLOCK > live)
        def _():
            slot = first + lax.broadcasted_iota(jnp.int32, (BLOCK, 1), 0)
            outs[span(b), :] = jnp.where(slot < live, outs[span(b), :].astype(jnp.float32), 0.0).astype(jnp.bfloat16)

        copy_out(b).start()

        def add_window(k, carry):
            base = pl.multiple_of(bounds[b] + k * WINDOW, 8)
            acc[pl.ds(base, WINDOW), :] += dot(window_hits(base, recv_rows[b]), outs[span(b), :])
            return carry

        lax.fori_loop(0, bounds[8 + b], add_window, 0)

    def block(b, carry):
        first = b * BLOCK
        before = jnp.maximum(first - HALF, 0)
        for c in range(pieces):
            silu_piece(c, first, g0, hid0)
        y0 = dot(hid0[...], w2[...])
        for c in range(pieces):
            silu_piece(c, first + HALF, g1, hid1)
            fetch_piece(c, first + BLOCK, g0)
            norm_piece(c, before, y1)
        y_next = dot(hid1[...], w2[...])
        for c in range(pieces):
            norm_piece(c, first, y0)
            fetch_piece(c, first + BLOCK + HALF, g1)
        y1[...] = y_next

        @pl.when(b > 0)
        def _():
            finish(b - 1)

        return carry

    lax.fori_loop(0, blocks, block, 0)
    for c in range(pieces):
        norm_piece(c, 4096 - HALF, y1)
    finish(blocks - 1)
    pre = node_part[...] + dot(acc[0:512, :].astype(jnp.bfloat16), nw1[512:1024, :])
    update = normed(dot(half_silu(0.5 * pre), nw2[...]) + nb2[...], ngain, nshift)
    node_out[...] = (node[...].astype(jnp.float32) + update).astype(jnp.bfloat16)
    for b in range(blocks):
        copy_out(b).wait()


VMEM = pl.BlockSpec(memory_space=pltpu.VMEM)
SMEM = pl.BlockSpec(memory_space=pltpu.SMEM)
HBM = pl.BlockSpec(memory_space=pltpu.HBM)


def shape(rows, columns, dtype):
    return jax.ShapeDtypeStruct((rows, columns), dtype)


def params(mib):
    return pltpu.CompilerParams(vmem_limit_bytes=mib << 20)


def cost(rows, deep):
    return pl.CostEstimate(flops=rows * deep * 1024, bytes_accessed=rows * 3072, transcendentals=0)


def on_device(
    node_feat, edge_feat, sender, receiver, send_list,
    edge_w1, edge_b1, edge_w2, edge_b2, edge_gain, edge_shift,
    node_w1, node_b1, node_w2, node_b2, node_gain, node_shift,
):
    core = lax.axis_index("region") & 1
    barrier = lax.optimization_barrier
    row = lambda a: a.reshape(1, -1)
    ids = jnp.arange(512, dtype=jnp.int32)
    pick = (send_list.reshape(256, 1) == ids[None, :]).astype(jnp.bfloat16)
    rows = dot(pick, node_feat).astype(jnp.bfloat16)
    recv_rows = receiver.reshape(4096 // BLOCK, 1, BLOCK)
    b1 = row(edge_b1)

    table = shape(ROWS * 4, 128, jnp.float32)
    bf16, f32 = jnp.bfloat16, jnp.float32
    in_hbm = lambda a: pltpu.with_memory_space_constraint(a, pltpu.HBM)

    held = ring_phase(node_feat[:COARSE_DEV], 0)
    held, rows, recv_rows = barrier((held, rows, recv_rows))
    rows = rows.reshape(8, 32, 512)
    up = shifted([rows[4], rows[6], rows[2]], 8)
    down = shifted([rows[5], rows[3], rows[7]], -8)
    held = ring_phase(held, 1)
    node_v, w1_v, edge_v, high, low_bits, ts, node_part, bounds = pl.pallas_call(
        first_kernel,
        in_specs=[HBM] * 4 + [VMEM] * 2,
        out_specs=[VMEM] * 7 + [SMEM],
        out_shape=[
            shape(512, 512, bf16), shape(1536, 512, bf16), shape(4096, 512, bf16),
            shape(640, 512, bf16), shape(640, 512, bf16), table, shape(512, 512, f32),
            jax.ShapeDtypeStruct((32,), jnp.int32),
        ],
        scratch_shapes=[pltpu.VMEM((512, 512), bf16), pltpu.SemaphoreType.DMA((4,))],
        compiler_params=params(8),
        cost_estimate=cost(1536, 512),
    )(in_hbm(node_feat), in_hbm(edge_w1), in_hbm(node_w1), in_hbm(edge_feat), row(node_b1), recv_rows)
    held, up, down, node_v, high, sender = barrier((held, up, down, node_v, high, sender))

    to_right = jnp.concatenate([rows[0], up[32:64], down[32:64]], 0)
    to_left = jnp.concatenate([rows[1], up[64:96], down[64:96]], 0)
    across = [(i, (i + 1) % 128 if i & 1 else (i - 1) % 128) for i in range(128)]
    beside = lax.ppermute(jnp.where(core == 1, to_right, to_left), "region", across)
    own = ring_phase(held, 2)
    part = pl.pallas_call(
        early_kernel,
        in_specs=[SMEM] + [VMEM] * 6,
        out_specs=VMEM,
        out_shape=shape(4096, 512, f32),
        compiler_params=params(8),
        cost_estimate=cost(4096, 768),
    )(bounds, recv_rows, edge_v, w1_v, b1, high, low_bits)

    right = jnp.where(core == 0, NEXT, SWAP)
    left = jnp.where(core == 0, SWAP, NEXT)
    starts = (right, left, left + 32, right + 64, UP, DOWN, right + 32, left + 64)
    h = sender - 2560
    slot = h >> 5
    start = jnp.broadcast_to(starts[0], sender.shape).astype(jnp.int32)
    for j in range(1, 8):
        start = jnp.where(slot == j, starts[j], start)
    place = jnp.where(
        sender < 512,
        sender,
        jnp.where(sender < 2560, OWN + coarse_places(sender - 512), start + (h & 31)),
    )
    place = jnp.pad(place * 4, (0, BLOCK))
    own, beside, part, place = barrier((own, beside, part, place))

    inside = jnp.where(core == 0, to_right, to_left)
    swapped = lax.ppermute(
        jnp.concatenate([own, inside], 0), "region", [(i, i ^ 1) for i in range(128)]
    )
    ts = pl.pallas_call(
        table_kernel,
        in_specs=[VMEM] * 6,
        out_specs=VMEM,
        out_shape=table,
        input_output_aliases={5: 0},
        compiler_params=params(8),
        cost_estimate=cost(1312, 512),
    )(own, up, down, beside, w1_v, ts)

    edge_out, node_out, _ = pl.pallas_call(
        layer_kernel,
        in_specs=[SMEM] * 2 + [VMEM] * 17,
        out_specs=[HBM, VMEM, VMEM],
        out_shape=[shape(4096, 512, bf16), shape(512, 512, bf16), table],
        input_output_aliases={7: 2},
        scratch_shapes=[
            pltpu.VMEM((HALF * 4, 128), f32),
            pltpu.VMEM((HALF * 4, 128), f32),
            pltpu.VMEM((HALF, 512), bf16),
            pltpu.VMEM((HALF, 512), bf16),
            pltpu.VMEM((HALF, 512), f32),
            pltpu.VMEM((640, 512), f32),
            pltpu.VMEM((4096, 512), bf16),
            pltpu.SemaphoreType.DMA((4096 // BLOCK,)),
        ],
        compiler_params=params(20),
    )(
        place, bounds, recv_rows, part, edge_v, node_v, swapped, ts, w1_v,
        edge_w2, row(edge_b2), row(edge_gain), row(edge_shift),
        node_part, node_w1, node_w2, row(node_b2), row(node_gain), row(node_shift),
    )
    return edge_out, node_out


def solution(mesh):
    sharded = {0: P("region", None), 1: P("region", None), 2: P("region"), 3: P("region"), 4: P("region", None, None)}
    in_specs = tuple(sharded.get(i, P()) for i in range(17))
    out_specs = (P("region", None), P("region", None))
    step = lambda *a: tuple(on_device(*a))
    return jax.shard_map(step, mesh=mesh, in_specs=in_specs, out_specs=out_specs, check_vma=False)
```

profile of v0, /device:TPU:1, one launch (start us, length us, event | category | flops | bytes accessed | tf_op | source)
XLA Modules:
  0.0 59.6 jit_solution(1014399263872753220)
XLA Ops:
  0.6 0.7 %slice.47 = bf16[16,512]{1,0:T(8,128)(2,1)S(1)} slice(bf16[512,512]{1,0:T(8,128)(2,1)} %node.1), slice={[0:16], [0:512]} | slice | bytes 32768 | tf_op jit(solution)/shard_map/slice | solution.py:296
  1.4 3.3 %collective-permute-start.2 = (bf16[16,512]{1,0:T(8,128)(2,1)S(1)}, bf16[16,512]{1,0:T(8,128)(2,1)S(1)}, u32[]{:S(2)}, u32[]{:S(2)}) collective-permute-start(bf16[16,512]{1,0:T(8,128)(2,1)S(1)} %slice.47), channel_id=1, source_target_pairs={{0,6},{1,97},{2,0},{3,99},{4,2},{5,101},{6,4},{7,103},{8,14},{9,10... | collective-permute-start | bytes 49160 | tf_op jit(solution)/shard_map/ppermute | solution.py:41
  4.6 0.5 collective-permute-start.1
  5.2 0.6 %collective-permute-start = (bf16[16,512]{1,0:T(8,128)(2,1)S(1)}, bf16[16,512]{1,0:T(8,128)(2,1)S(1)}, u32[]{:S(2)}, u32[]{:S(2)}) collective-permute-start(bf16[16,512]{1,0:T(8,128)(2,1)S(1)} %slice.47), channel_id=1, source_target_pairs={{0,2},{1,33},{2,4},{3,35},{4,6},{5,37},{6,0},{7,39},{8,10},{9,41},... | collective-permute-start | bytes 49160 | tf_op jit(solution)/shard_map/ppermute | solution.py:41
  5.8 0.8 %eq.63 = s32[256]{0:T(256)S(1)} reshape(s32[1,8,32]{2,1,0:T(8,128)} %param.21) | data formatting | bytes 2048 | tf_op jit(solution)/shard_map/eq | solution.py:287
  6.5 1.4 %convolution_convert_fusion = bf16[256,512]{1,0:T(8,128)(2,1)S(1)} fusion(bf16[512,512]{1,0:T(8,128)(2,1)} %node.1, s32[256]{0:T(256)S(1)} %eq.63), kind=kOutput, calls=%fused_computation | convolution fusion | flops 134479872 | bytes 787456 | tf_op jit(solution)/shard_map/dot_general | solution.py:72
  8.0 0.8 %collective-permute-done.1 = bf16[16,512]{1,0:T(8,128)(2,1)S(1)} collective-permute-done((bf16[16,512]{1,0:T(8,128)(2,1)S(1)}, bf16[16,512]{1,0:T(8,128)(2,1)S(1)}, u32[]{:S(2)}, u32[]{:S(2)}) %collective-permute-start.1) | collective-permute-done | bytes 16416 | tf_op jit(solution)/shard_map/ppermute | solution.py:41
  8.7 0.2 collective-permute-done
  9.0 3.8 %collective-permute-start.5 = (bf16[64,512]{1,0:T(8,128)(2,1)S(1)}, bf16[64,512]{1,0:T(8,128)(2,1)S(1)}, u32[]{:S(2)}, u32[]{:S(2)}) collective-permute-start(bf16[64,512]{1,0:T(8,128)(2,1)S(1)} %pad_maximum_fusion.7), channel_id=1, source_target_pairs={{0,24},{1,7},{2,26},{3,1},{4,28},{5,3},{6,30},{7,5},{8,0},{9,15},{... | collective-permute-start | bytes 196616 | tf_op jit(solution)/shard_map/ppermute | solution.py:41
  12.7 0.7 %collective-permute-start.3 = (bf16[64,512]{1,0:T(8,128)(2,1)S(1)}, bf16[64,512]{1,0:T(8,128)(2,1)S(1)}, u32[]{:S(2)}, u32[]{:S(2)}) collective-permute-start(bf16[64,512]{1,0:T(8,128)(2,1)S(1)} %pad_maximum_fusion.7), channel_id=1, source_target_pairs={{0,8},{1,3},{2,10},{3,5},{4,12},{5,7},{6,14},{7,1},{8,16},{9,11},{... | collective-permute-start | bytes 196616 | tf_op jit(solution)/shard_map/ppermute | solution.py:41
  13.5 1.4 %collective-permute-start.6 = (bf16[96,512]{1,0:T(8,128)(2,1)S(1)}, bf16[96,512]{1,0:T(8,128)(2,1)S(1)}, u32[]{:S(2)}, u32[]{:S(2)}) collective-permute-start(bf16[96,512]{1,0:T(8,128)(2,1)S(1)} %pad_maximum_fusion.3), channel_id=1, source_target_pairs={{0,8},{1,9},{2,10},{3,11},{4,12},{5,13},{6,14},{7,15},{8,16},{9,17... | collective-permute-start | bytes 294920 | tf_op jit(solution)/shard_map/ppermute | solution.py:46
  14.8 3.6 %collective-permute-start.7 = (bf16[96,512]{1,0:T(8,128)(2,1)S(1)}, bf16[96,512]{1,0:T(8,128)(2,1)S(1)}, u32[]{:S(2)}, u32[]{:S(2)}) collective-permute-start(bf16[96,512]{1,0:T(8,128)(2,1)S(1)} %pad_maximum_fusion.4), channel_id=1, source_target_pairs={{0,120},{1,121},{2,122},{3,123},{4,124},{5,125},{6,126},{7,127},{8... | collective-permute-start | bytes 294920 | tf_op jit(solution)/shard_map/ppermute | solution.py:46
  18.4 0.7 %copy-done.3 = s32[4096]{0:T(1024)S(1)} copy-done((s32[4096]{0:T(1024)S(1)}, s32[4096]{0:T(1024)}, u32[]{:S(2)}) %copy-start.3) | copy-done | bytes 16408
  19.1 0.7 %copy-done.12 = f32[512]{0:T(512)S(1)} copy-done((f32[512]{0:T(512)S(1)}, f32[512]{0:T(512)}, u32[]{:S(2)}) %copy-start.12) | copy-done | bytes 2072
  19.8 3.7 %shard_map.176 = (bf16[512,512]{1,0:T(8,128)(2,1)S(1)}, bf16[1536,512]{1,0:T(8,128)(2,1)S(1)}, bf16[4096,512]{1,0:T(8,128)(2,1)S(1)}, bf16[640,512]{1,0:T(8,128)...) custom-call(bf16[512,512]{1,0:T(8,128)(2,1)} %node.1, ...), custom_call_target="tpu_custom_call" | custom-call | flops 805306368 | bytes 4718592 | tf_op jit(solution)/shard_map/pallas_call | solution.py:302
  23.5 0.1 collective-permute-start.10
  23.6 0.1 collective-permute-start.9
  23.7 1.4 %collective-permute-start.8 = (bf16[256,512]{1,0:T(8,128)(2,1)S(1)}, bf16[256,512]{1,0:T(8,128)(2,1)S(1)}, u32[]{:S(2)}, u32[]{:S(2)}) collective-permute-start(bf16[256,512]{1,0:T(8,128)(2,1)S(1)} %pad_maximum_fusion.2), channel_id=1, source_target_pairs={{0,32},{1,9},{2,34},{3,11},{4,36},{5,13},{6,38},{7,15},{8,40},{9,1... | collective-permute-start | bytes 786440 | tf_op jit(solution)/shard_map/ppermute | solution.py:41
  25.2 5.9 %collective-permute-start.11 = (bf16[96,512]{1,0:T(8,128)(2,1)S(1)}, bf16[96,512]{1,0:T(8,128)(2,1)S(1)}, u32[]{:S(2)}, u32[]{:S(2)}) collective-permute-start(bf16[96,512]{1,0:T(8,128)(2,1)S(1)} %get-tuple-element.57), channel_id=1, source_target_pairs={{0,127},{1,2},{2,1},{3,4},{4,3},{5,6},{6,5},{7,8},{8,7},{9,10},{10... | collective-permute-start | bytes 294920 | tf_op jit(solution)/shard_map/ppermute | solution.py:320
  31.1 5.5 %shard_map.177.part = f32[4096,512]{1,0:T(8,128)S(1)} custom-call(s32[32]{0:T(128)S(1)} %get-tuple-element.33.bounds, s32[8,1,512]{2,1,0:T(1,128)S(1)} %bitcast.11, bf16[4096,512]{1,0:T(8,128)(2,1)S(1)} %get-tuple-element.34.edge, bf16[1536,512]{1,0:T(8,128)(2,1)S(1)} %get-tuple-element.35.w1, f32[1,512]{1,0:T(1,128)S(1)} %bitcast.13, ...), custom_call_target="tpu_custom_call" | custom-call | flops 3221225472 | bytes 12582912 | tf_op jit(solution)/shard_map/pallas_call | solution.py:322
  36.6 0.1 pad_maximum_fusion.1.own
  36.7 0.1 pad_maximum_fusion
  36.8 4.9 %collective-permute-start.12 = (bf16[1120,512]{1,0:T(8,128)(2,1)S(1)}, bf16[1120,512]{1,0:T(8,128)(2,1)S(1)}, u32[]{:S(2)}, u32[]{:S(2)}) collective-permute-start(bf16[1120,512]{1,0:T(8,128)(2,1)S(1)} %pad_maximum_fusion), channel_id=1, source_target_pairs={{0,1},{1,0},{2,3},{3,2},{4,5},{5,4},{6,7},{7,6},{8,9},{9,8},{10,11... | collective-permute-start | bytes 3440648 | tf_op jit(solution)/shard_map/ppermute | solution.py:348
  41.7 0.0 copy-start.6
  41.7 0.0 copy-start.7
  41.7 0.0 copy-start.8
  41.7 0.0 copy-start.9
  41.7 0.0 copy-start.10
  41.8 0.0 copy-start.11
  41.8 0.9 %shard_map.178.old_ts = f32[11776,128]{1,0:T(8,128)S(1)} custom-call(bf16[1024,512]{1,0:T(8,128)(2,1)S(1)} %pad_maximum_fusion.1.own, bf16[96,512]{1,0:T(8,128)(2,1)S(1)} %collective-permute-done.6.up, bf16[96,512]{1,0:T(8,128)(2,1)S(1)} %collective-permute-done.7.down, ...), custom_call_target="tpu_custom_call", output_to_operand_aliasing={{}: (5, {})} | custom-call | flops 687865856 | bytes 4030464 | tf_op jit(solution)/shard_map/pallas_call | solution.py:351
  42.7 1.4 %collective-permute-done.12.swapped = bf16[1120,512]{1,0:T(8,128)(2,1)S(1)} collective-permute-done((bf16[1120,512]{1,0:T(8,128)(2,1)S(1)}, bf16[1120,512]{1,0:T(8,128)(2,1)S(1)}, u32[]{:S(2)}, u32[]{:S(2)}) %collective-permute-start.12) | collective-permute-done | bytes 1146912 | tf_op jit(solution)/shard_map/ppermute | solution.py:348
  44.2 15.5 %shard_map.179 = (bf16[4096,512]{1,0:T(8,128)(2,1)}, bf16[512,512]{1,0:T(8,128)(2,1)}, f32[11776,128]{1,0:T(8,128)S(1)}) custom-call(s32[4608]{0:T(1024)S(1)} %pad.4.send_ref, s32[32]{0:T(128)S(1)} %get-tuple-element.33.bounds, s32[8,1,512]{2,1,0:T(1,128)S(1)} %bitcast.12, f32[4096,512]{1,0:T(8,128)S(1)} %shard_map.177.part, ...), custom_call_target="tpu_custom_call", output_to_operand_aliasing={{2}: (7, {})} | custom-call | tf_op jit(solution)/shard_map/pallas_call | solution.py:361
  (40 shorter events, 0.2 us)
Async XLA Ops:
  1.4 6.6 %collective-permute-start.2 = (bf16[16,512]{1,0:T(8,128)(2,1)S(1)}, bf16[16,512]{1,0:T(8,128)(2,1)S(1)}, u32[]{:S(2)}, u32[]{:S(2)}) collective-permute-start(bf16[16,512]{1,0:T(8,128)(2,1)S(1)} %slice.47), channel_id=1, source_target_pairs={{0,6},{1,97},{2,0},{3,99},{4,2},{5,101},{6,4},{7,103},{8,14},{9,10... | collective-permute-start | bytes 49160 | tf_op jit(solution)/shard_map/ppermute | solution.py:41
  4.6 4.1 %collective-permute-start.1 = (bf16[16,512]{1,0:T(8,128)(2,1)S(1)}, bf16[16,512]{1,0:T(8,128)(2,1)S(1)}, u32[]{:S(2)}, u32[]{:S(2)}) collective-permute-start(bf16[16,512]{1,0:T(8,128)(2,1)S(1)} %slice.47), channel_id=1, source_target_pairs={{0,4},{1,65},{2,6},{3,67},{4,0},{5,69},{6,2},{7,71},{8,12},{9,73},... | collective-permute-start | bytes 49160 | tf_op jit(solution)/shard_map/ppermute | solution.py:41
  5.2 3.8 %collective-permute-start = (bf16[16,512]{1,0:T(8,128)(2,1)S(1)}, bf16[16,512]{1,0:T(8,128)(2,1)S(1)}, u32[]{:S(2)}, u32[]{:S(2)}) collective-permute-start(bf16[16,512]{1,0:T(8,128)(2,1)S(1)} %slice.47), channel_id=1, source_target_pairs={{0,2},{1,33},{2,4},{3,35},{4,6},{5,37},{6,0},{7,39},{8,10},{9,41},... | collective-permute-start | bytes 49160 | tf_op jit(solution)/shard_map/ppermute | solution.py:41
  9.0 14.5 %collective-permute-start.5 = (bf16[64,512]{1,0:T(8,128)(2,1)S(1)}, bf16[64,512]{1,0:T(8,128)(2,1)S(1)}, u32[]{:S(2)}, u32[]{:S(2)}) collective-permute-start(bf16[64,512]{1,0:T(8,128)(2,1)S(1)} %pad_maximum_fusion.7), channel_id=1, source_target_pairs={{0,24},{1,7},{2,26},{3,1},{4,28},{5,3},{6,30},{7,5},{8,0},{9,15},{... | collective-permute-start | bytes 196616 | tf_op jit(solution)/shard_map/ppermute | solution.py:41
  12.7 10.7 %collective-permute-start.4 = (bf16[64,512]{1,0:T(8,128)(2,1)S(1)}, bf16[64,512]{1,0:T(8,128)(2,1)S(1)}, u32[]{:S(2)}, u32[]{:S(2)}) collective-permute-start(bf16[64,512]{1,0:T(8,128)(2,1)S(1)} %pad_maximum_fusion.7), channel_id=1, source_target_pairs={{0,16},{1,5},{2,18},{3,7},{4,20},{5,1},{6,22},{7,3},{8,24},{9,13},... | collective-permute-start | bytes 196616 | tf_op jit(solution)/shard_map/ppermute | solution.py:41
  12.7 10.8 %collective-permute-start.3 = (bf16[64,512]{1,0:T(8,128)(2,1)S(1)}, bf16[64,512]{1,0:T(8,128)(2,1)S(1)}, u32[]{:S(2)}, u32[]{:S(2)}) collective-permute-start(bf16[64,512]{1,0:T(8,128)(2,1)S(1)} %pad_maximum_fusion.7), channel_id=1, source_target_pairs={{0,8},{1,3},{2,10},{3,5},{4,12},{5,7},{6,14},{7,1},{8,16},{9,11},{... | collective-permute-start | bytes 196616 | tf_op jit(solution)/shard_map/ppermute | solution.py:41
  13.5 10.1 %collective-permute-start.6 = (bf16[96,512]{1,0:T(8,128)(2,1)S(1)}, bf16[96,512]{1,0:T(8,128)(2,1)S(1)}, u32[]{:S(2)}, u32[]{:S(2)}) collective-permute-start(bf16[96,512]{1,0:T(8,128)(2,1)S(1)} %pad_maximum_fusion.3), channel_id=1, source_target_pairs={{0,8},{1,9},{2,10},{3,11},{4,12},{5,13},{6,14},{7,15},{8,16},{9,17... | collective-permute-start | bytes 294920 | tf_op jit(solution)/shard_map/ppermute | solution.py:46
  14.8 8.7 %collective-permute-start.7 = (bf16[96,512]{1,0:T(8,128)(2,1)S(1)}, bf16[96,512]{1,0:T(8,128)(2,1)S(1)}, u32[]{:S(2)}, u32[]{:S(2)}) collective-permute-start(bf16[96,512]{1,0:T(8,128)(2,1)S(1)} %pad_maximum_fusion.4), channel_id=1, source_target_pairs={{0,120},{1,121},{2,122},{3,123},{4,124},{5,125},{6,126},{7,127},{8... | collective-permute-start | bytes 294920 | tf_op jit(solution)/shard_map/ppermute | solution.py:46
  18.4 0.7 %copy-start.3 = (s32[4096]{0:T(1024)S(1)}, s32[4096]{0:T(1024)}, u32[]{:S(2)}) copy-start(s32[4096]{0:T(1024)} %param.20) | copy-start | bytes 49156
  19.1 0.7 %copy-start.12 = (f32[512]{0:T(512)S(1)}, f32[512]{0:T(512)}, u32[]{:S(2)}) copy-start(f32[512]{0:T(512)} %param.29) | copy-start | bytes 6148
  19.8 5.3 %copy-start.13 = (s32[4096]{0:T(1024)S(1)}, s32[4096]{0:T(1024)}, u32[]{:S(2)}) copy-start(s32[4096]{0:T(1024)} %param.19) | copy-start | bytes 49156
  19.8 11.3 %copy-start.5 = (f32[512]{0:T(512)S(1)}, f32[512]{0:T(512)}, u32[]{:S(2)}) copy-start(f32[512]{0:T(512)} %param.23) | copy-start | bytes 6148
  23.5 13.0 %collective-permute-start.10 = (bf16[256,512]{1,0:T(8,128)(2,1)S(1)}, bf16[256,512]{1,0:T(8,128)(2,1)S(1)}, u32[]{:S(2)}, u32[]{:S(2)}) collective-permute-start(bf16[256,512]{1,0:T(8,128)(2,1)S(1)} %pad_maximum_fusion.2), channel_id=1, source_target_pairs={{0,96},{1,25},{2,98},{3,27},{4,100},{5,29},{6,102},{7,31},{8,104},... | collective-permute-start | bytes 786440 | tf_op jit(solution)/shard_map/ppermute | solution.py:41
  23.6 12.9 %collective-permute-start.9 = (bf16[256,512]{1,0:T(8,128)(2,1)S(1)}, bf16[256,512]{1,0:T(8,128)(2,1)S(1)}, u32[]{:S(2)}, u32[]{:S(2)}) collective-permute-start(bf16[256,512]{1,0:T(8,128)(2,1)S(1)} %pad_maximum_fusion.2), channel_id=1, source_target_pairs={{0,64},{1,17},{2,66},{3,19},{4,68},{5,21},{6,70},{7,23},{8,72},{9,... | collective-permute-start | bytes 786440 | tf_op jit(solution)/shard_map/ppermute | solution.py:41
  23.7 12.9 %collective-permute-start.8 = (bf16[256,512]{1,0:T(8,128)(2,1)S(1)}, bf16[256,512]{1,0:T(8,128)(2,1)S(1)}, u32[]{:S(2)}, u32[]{:S(2)}) collective-permute-start(bf16[256,512]{1,0:T(8,128)(2,1)S(1)} %pad_maximum_fusion.2), channel_id=1, source_target_pairs={{0,32},{1,9},{2,34},{3,11},{4,36},{5,13},{6,38},{7,15},{8,40},{9,1... | collective-permute-start | bytes 786440 | tf_op jit(solution)/shard_map/ppermute | solution.py:41
  25.2 11.5 %collective-permute-start.11 = (bf16[96,512]{1,0:T(8,128)(2,1)S(1)}, bf16[96,512]{1,0:T(8,128)(2,1)S(1)}, u32[]{:S(2)}, u32[]{:S(2)}) collective-permute-start(bf16[96,512]{1,0:T(8,128)(2,1)S(1)} %get-tuple-element.57), channel_id=1, source_target_pairs={{0,127},{1,2},{2,1},{3,4},{4,3},{5,6},{6,5},{7,8},{8,7},{9,10},{10... | collective-permute-start | bytes 294920 | tf_op jit(solution)/shard_map/ppermute | solution.py:320
  36.8 7.3 %collective-permute-start.12 = (bf16[1120,512]{1,0:T(8,128)(2,1)S(1)}, bf16[1120,512]{1,0:T(8,128)(2,1)S(1)}, u32[]{:S(2)}, u32[]{:S(2)}) collective-permute-start(bf16[1120,512]{1,0:T(8,128)(2,1)S(1)} %pad_maximum_fusion), channel_id=1, source_target_pairs={{0,1},{1,0},{2,3},{3,2},{4,5},{5,4},{6,7},{7,6},{8,9},{9,8},{10,11... | collective-permute-start | bytes 3440648 | tf_op jit(solution)/shard_map/ppermute | solution.py:348
  41.7 2.4 %copy-start = (bf16[1024,512]{1,0:T(8,128)(2,1)S(1)}, bf16[1024,512]{1,0:T(8,128)(2,1)}, u32[]{:S(2)}) copy-start(bf16[1024,512]{1,0:T(8,128)(2,1)} %nw1.3) | copy-start | bytes 3145732
  41.7 2.4 %copy-start.1 = (bf16[512,512]{1,0:T(8,128)(2,1)S(1)}, bf16[512,512]{1,0:T(8,128)(2,1)}, u32[]{:S(2)}) copy-start(bf16[512,512]{1,0:T(8,128)(2,1)} %w2.1) | copy-start | bytes 1572868
  41.7 2.4 %copy-start.2 = (bf16[512,512]{1,0:T(8,128)(2,1)S(1)}, bf16[512,512]{1,0:T(8,128)(2,1)}, u32[]{:S(2)}) copy-start(bf16[512,512]{1,0:T(8,128)(2,1)} %nw2.1) | copy-start | bytes 1572868
  41.7 2.4 %copy-start.4 = (s32[4096]{0:T(1024)S(1)}, s32[4096]{0:T(1024)}, u32[]{:S(2)}) copy-start(s32[4096]{0:T(1024)} %param.20) | copy-start | bytes 49156
  41.7 2.4 %copy-start.6 = (f32[512]{0:T(512)S(1)}, f32[512]{0:T(512)}, u32[]{:S(2)}) copy-start(f32[512]{0:T(512)} %param.25) | copy-start | bytes 6148
  41.7 2.4 %copy-start.7 = (f32[512]{0:T(512)S(1)}, f32[512]{0:T(512)}, u32[]{:S(2)}) copy-start(f32[512]{0:T(512)} %param.26) | copy-start | bytes 6148
  41.7 2.4 %copy-start.8 = (f32[512]{0:T(512)S(1)}, f32[512]{0:T(512)}, u32[]{:S(2)}) copy-start(f32[512]{0:T(512)} %param.27) | copy-start | bytes 6148
  41.7 2.4 %copy-start.9 = (f32[512]{0:T(512)S(1)}, f32[512]{0:T(512)}, u32[]{:S(2)}) copy-start(f32[512]{0:T(512)} %param.31) | copy-start | bytes 6148
  41.7 2.4 %copy-start.10 = (f32[512]{0:T(512)S(1)}, f32[512]{0:T(512)}, u32[]{:S(2)}) copy-start(f32[512]{0:T(512)} %param.32) | copy-start | bytes 6148
  41.8 2.4 %copy-start.11 = (f32[512]{0:T(512)S(1)}, f32[512]{0:T(512)}, u32[]{:S(2)}) copy-start(f32[512]{0:T(512)} %param.33) | copy-start | bytes 6148
where the time goes:
time: 60.1 us; the launch traced here: 59.6 us
  starting transfers between devices  26.1 us (43%)
  Pallas kernels  25.5 us (42%)
  local copies, waits for them, and re-layouts  2.98 us (5%)
  waiting for transfers between devices  2.43 us (4%)
  matrix products  1.39 us (2%)
  between operations  0.95 us (2%)
    pallas_call x1, Pallas kernels, on_device(): pl.pallas_call(layer_kernel, in_specs=[SMEM] * 2 + [VMEM] * 17, out_specs...  15.5 us
    ppermute x9, starting transfers between devices, ring_phase(): lax.ppermute(held, 'region', ring_route(phase, k))  10.4 us
    ppermute x1, starting transfers between devices, on_device(): lax.ppermute(jnp.where(core == 1, to_right, to_left), 'region', across)  5.86 us
    pallas_call x1, Pallas kernels, on_device(): pl.pallas_call(early_kernel, in_specs=[SMEM] + [VMEM] * 6, out_specs=VMEM...  5.48 us
    ppermute x1, starting transfers between devices, on_device(): lax.ppermute(jnp.concatenate([own, inside], 0), 'region', [(i, i ^ 1) for...  4.92 us
    ppermute x2, starting transfers between devices, shifted(): lax.ppermute(jnp.concatenate(blocks, 0), 'region', linear_route(step))  4.92 us
    pallas_call x1, Pallas kernels, on_device(): pl.pallas_call(first_kernel, in_specs=[HBM] * 4 + [VMEM] * 2, out_specs=[...  3.66 us
    unnamed x28, local copies, waits for them, and re-layouts  1.46 us
  transfers between devices with their start and end apart: 13, of which 3 were waited for; matrix products, arithmetic and copies ran while one was open for 4% of the time, Pallas kernels for 17%

commit v1 on v0

--- a/solution.py
+++ b/solution.py
@@ -86,23 +86,28 @@
 
 
 def first_kernel(
-    node, w1, nw1, edge, nb1, recv_rows,
-    node_v, w1_v, edge_v, high, low_bits, ts, node_part, bounds,
+    node, w1, nw1, recv_rows, picks,
+    node_v, w1_v, recv_v, high, low_bits, ts, node_part, rows, bounds,
     nw_top, sems,
 ):
-    moves = [(node, node_v), (w1, w1_v), (nw1.at[0:512, :], nw_top), (edge, edge_v)]
+    moves = [(recv_rows, recv_v), (node, node_v), (w1, w1_v), (nw1.at[0:512, :], nw_top)]
     copies = [pltpu.make_async_copy(a, b, sems.at[i]) for i, (a, b) in enumerate(moves)]
     for copy in copies:
         copy.start()
-    recv = recv_rows[:, 0, :]
-    used = jnp.where(recv < 512, 1, 0)
-    bounds[16] = jnp.sum(used)
+    ids = lax.broadcasted_iota(jnp.int32, (512, 256), 0)
+    chosen = jnp.where(ids == picks[...], 1.0, 0.0).astype(jnp.bfloat16)
+    copies[0].wait()
+    recv = recv_v[:, 0, :]
+    bounds[16] = jnp.sum(jnp.where(recv < 512, 1, 0))
     for b in range(4096 // BLOCK):
         low = jnp.min(recv[b : b + 1, :]) >> 3 << 3
         bounds[b] = low
         bounds[8 + b] = (jnp.max(recv[b : b + 1, :]) - low) // WINDOW + 1
-    copies[0].wait()
     copies[1].wait()
+    rows[...] = lax.dot_general(
+        chosen, node_v[...], (((0,), (0,)), ((), ())), preferred_element_type=jnp.float32
+    ).astype(jnp.bfloat16)
+    copies[2].wait()
     tr = 0.5 * dot(node_v[...], w1_v[1024:1536, :])
     top = tr.astype(jnp.bfloat16)
     high[0:512, :] = top
@@ -111,17 +116,27 @@
     high[512:, :] = pad
     low_bits[512:, :] = pad
     project(node_v, 0, 512, 0, w1_v, ts)
-    copies[2].wait()
-    node_part[...] = dot(node_v[...], nw_top[...]) + nb1[...]
     copies[3].wait()
-
-
-def early_kernel(bounds, recv_rows, edge, w1, b1, high, low_bits, part):
+    node_part[...] = dot(node_v[...], nw_top[...])
+
+
+def early_kernel(bounds, recv_rows, edge, w1, b1, high, low_bits, part, edge_v, sems):
+    def span_of(b):
+        return pl.ds(pl.multiple_of(b * BLOCK, BLOCK), BLOCK)
+
+    def copy(b):
+        return pltpu.make_async_copy(edge.at[span_of(b), :], edge_v.at[span_of(b), :], sems.at[b])
+
+    for b in range(4096 // BLOCK):
+        copy(b).start()
+
     def pair(p, carry):
+        copy(p * 2).wait()
+        copy(p * 2 + 1).wait()
         spreads = []
         for i in range(2):
             b = p * 2 + i
-            span = pl.ds(pl.multiple_of(b * BLOCK, BLOCK), BLOCK)
+            span = span_of(b)
 
             def spread(k, b=b):
                 base = pl.multiple_of(bounds[b] + k * WINDOW, 8)
@@ -132,7 +147,7 @@
                     (((0,), (0,)), ((), ())), preferred_element_type=jnp.float32,
                 )
 
-            part[span, :] = 0.5 * (dot(edge[span, :], w1[0:512, :]) + b1[...]) + spread(0)
+            part[span, :] = 0.5 * (dot(edge_v[span, :], w1[0:512, :]) + b1[...]) + spread(0)
             spreads.append((b, span, spread))
 
         for b, span, spread in spreads:
@@ -147,18 +162,17 @@
     lax.fori_loop(0, 4096 // BLOCK // 2, pair, 0)
 
 
-def table_kernel(own, up, down, beside, w1, old_ts, ts):
+def table_kernel(own, up, down, w1, old_ts, ts):
     del old_ts
     project(own, 0, 1024, OWN, w1, ts)
     project(up, 0, 96, UP, w1, ts)
     project(down, 0, 96, DOWN, w1, ts)
-    project(beside, 0, 96, NEXT, w1, ts)
 
 
 def layer_kernel(
     send_ref, bounds,
-    recv_rows, part, edge, node, swapped, old_ts, w1, w2, b2, gain, shift,
-    node_part, nw1, nw2, nb2, ngain, nshift,
+    recv_rows, part, edge, node, swapped, beside, old_ts, w1, w2, b2, gain, shift,
+    node_part, nw1, nb1, nw2, nb2, ngain, nshift,
     edge_out, node_out, ts,
     g0, g1, hid0, hid1, y1, acc, outs, out_sems,
 ):
@@ -177,14 +191,14 @@
 
     project(swapped, 0, 1024, OTHER, w1, ts)
     project(swapped, 1024, 96, SWAP, w1, ts)
+    project(beside, 0, 96, NEXT, w1, ts)
     acc[...] = jnp.zeros_like(acc)
     y1[...] = jnp.zeros_like(y1)
 
     def fetch16(i, carry):
         for e in range(16):
-            for g, at in ((g0, 0), (g1, HALF)):
-                s = pl.multiple_of(send_ref[at + i * 16 + e], 4)
-                g[pl.ds(pl.multiple_of(i * 64 + e * 4, 4), 4), :] = ts[pl.ds(s, 4), :]
+            s = pl.multiple_of(send_ref[i * 16 + e], 4)
+            g0[pl.ds(pl.multiple_of(i * 64 + e * 4, 4), 4), :] = ts[pl.ds(s, 4), :]
         return carry
 
     lax.fori_loop(0, HALF // 16, fetch16, 0)
@@ -230,6 +244,7 @@
         before = jnp.maximum(first - HALF, 0)
         for c in range(pieces):
             silu_piece(c, first, g0, hid0)
+            fetch_piece(c, first + HALF, g1)
         y0 = dot(hid0[...], w2[...])
         for c in range(pieces):
             silu_piece(c, first + HALF, g1, hid1)
@@ -238,7 +253,6 @@
         y_next = dot(hid1[...], w2[...])
         for c in range(pieces):
             norm_piece(c, first, y0)
-            fetch_piece(c, first + BLOCK + HALF, g1)
         y1[...] = y_next
 
         @pl.when(b > 0)
@@ -247,11 +261,22 @@
 
         return carry
 
-    lax.fori_loop(0, blocks, block, 0)
-    for c in range(pieces):
-        norm_piece(c, 4096 - HALF, y1)
-    finish(blocks - 1)
-    pre = node_part[...] + dot(acc[0:512, :].astype(jnp.bfloat16), nw1[512:1024, :])
+    busy = (live + BLOCK - 1) // BLOCK
+    lax.fori_loop(0, busy, block, 0)
+
+    @pl.when(busy > 0)
+    def _():
+        for c in range(pieces):
+            norm_piece(c, busy * BLOCK - HALF, y1)
+        finish(busy - 1)
+
+    def empty(b, carry):
+        outs[span(b), :] = jnp.zeros((BLOCK, 512), jnp.bfloat16)
+        copy_out(b).start()
+        return carry
+
+    lax.fori_loop(busy, blocks, empty, 0)
+    pre = node_part[...] + dot(acc[0:512, :].astype(jnp.bfloat16), nw1[512:1024, :]) + nb1[...]
     update = normed(dot(half_silu(0.5 * pre), nw2[...]) + nb2[...], ngain, nshift)
     node_out[...] = (node[...].astype(jnp.float32) + update).astype(jnp.bfloat16)
     for b in range(blocks):
@@ -283,9 +308,7 @@
     core = lax.axis_index("region") & 1
     barrier = lax.optimization_barrier
     row = lambda a: a.reshape(1, -1)
-    ids = jnp.arange(512, dtype=jnp.int32)
-    pick = (send_list.reshape(256, 1) == ids[None, :]).astype(jnp.bfloat16)
-    rows = dot(pick, node_feat).astype(jnp.bfloat16)
+    picks = send_list.reshape(1, 256)
     recv_rows = receiver.reshape(4096 // BLOCK, 1, BLOCK)
     b1 = row(edge_b1)
 
@@ -294,39 +317,36 @@
     in_hbm = lambda a: pltpu.with_memory_space_constraint(a, pltpu.HBM)
 
     held = ring_phase(node_feat[:COARSE_DEV], 0)
-    held, rows, recv_rows = barrier((held, rows, recv_rows))
-    rows = rows.reshape(8, 32, 512)
-    up = shifted([rows[4], rows[6], rows[2]], 8)
-    down = shifted([rows[5], rows[3], rows[7]], -8)
+    held, picks = barrier((held, picks))
     held = ring_phase(held, 1)
-    node_v, w1_v, edge_v, high, low_bits, ts, node_part, bounds = pl.pallas_call(
+    node_v, w1_v, recv_v, high, low_bits, ts, node_part, rows, bounds = pl.pallas_call(
         first_kernel,
-        in_specs=[HBM] * 4 + [VMEM] * 2,
-        out_specs=[VMEM] * 7 + [SMEM],
+        in_specs=[HBM] * 4 + [VMEM],
+        out_specs=[VMEM] * 8 + [SMEM],
         out_shape=[
-            shape(512, 512, bf16), shape(1536, 512, bf16), shape(4096, 512, bf16),
-            shape(640, 512, bf16), shape(640, 512, bf16), table, shape(512, 512, f32),
+            shape(512, 512, bf16), shape(1536, 512, bf16), jax.ShapeDtypeStruct(recv_rows.shape, jnp.int32),
+            shape(640, 512, bf16), shape(640, 512, bf16), table, shape(512, 512, f32), shape(256, 512, bf16),
             jax.ShapeDtypeStruct((32,), jnp.int32),
         ],
         scratch_shapes=[pltpu.VMEM((512, 512), bf16), pltpu.SemaphoreType.DMA((4,))],
         compiler_params=params(8),
-        cost_estimate=cost(1536, 512),
-    )(in_hbm(node_feat), in_hbm(edge_w1), in_hbm(node_w1), in_hbm(edge_feat), row(node_b1), recv_rows)
-    held, up, down, node_v, high, sender = barrier((held, up, down, node_v, high, sender))
-
-    to_right = jnp.concatenate([rows[0], up[32:64], down[32:64]], 0)
-    to_left = jnp.concatenate([rows[1], up[64:96], down[64:96]], 0)
-    across = [(i, (i + 1) % 128 if i & 1 else (i - 1) % 128) for i in range(128)]
-    beside = lax.ppermute(jnp.where(core == 1, to_right, to_left), "region", across)
+        cost_estimate=cost(1792, 512),
+    )(in_hbm(node_feat), in_hbm(edge_w1), in_hbm(node_w1), in_hbm(recv_rows), picks)
+    held, rows, node_v, high, sender = barrier((held, rows, node_v, high, sender))
+
+    rows = rows.reshape(8, 32, 512)
+    up = shifted([rows[4], rows[6], rows[2]], 8)
+    down = shifted([rows[5], rows[3], rows[7]], -8)
     own = ring_phase(held, 2)
-    part = pl.pallas_call(
+    part, edge_v = pl.pallas_call(
         early_kernel,
-        in_specs=[SMEM] + [VMEM] * 6,
-        out_specs=VMEM,
-        out_shape=shape(4096, 512, f32),
+        in_specs=[SMEM, VMEM, HBM] + [VMEM] * 4,
+        out_specs=[VMEM, VMEM],
+        out_shape=[shape(4096, 512, f32), shape(4096, 512, bf16)],
+        scratch_shapes=[pltpu.SemaphoreType.DMA((4096 // BLOCK,))],
         compiler_params=params(8),
         cost_estimate=cost(4096, 768),
-    )(bounds, recv_rows, edge_v, w1_v, b1, high, low_bits)
+    )(bounds, recv_v, in_hbm(edge_feat), w1_v, b1, high, low_bits)
 
     right = jnp.where(core == 0, NEXT, SWAP)
     left = jnp.where(core == 0, SWAP, NEXT)
@@ -342,28 +362,32 @@
         jnp.where(sender < 2560, OWN + coarse_places(sender - 512), start + (h & 31)),
     )
     place = jnp.pad(place * 4, (0, BLOCK))
-    own, beside, part, place = barrier((own, beside, part, place))
-
+    own, up, down, part, place = barrier((own, up, down, part, place))
+
+    to_right = jnp.concatenate([rows[0], up[32:64], down[32:64]], 0)
+    to_left = jnp.concatenate([rows[1], up[64:96], down[64:96]], 0)
     inside = jnp.where(core == 0, to_right, to_left)
     swapped = lax.ppermute(
         jnp.concatenate([own, inside], 0), "region", [(i, i ^ 1) for i in range(128)]
     )
+    across = [(i, (i + 1) % 128 if i & 1 else (i - 1) % 128) for i in range(128)]
+    beside = lax.ppermute(jnp.where(core == 1, to_right, to_left), "region", across)
     ts = pl.pallas_call(
         table_kernel,
-        in_specs=[VMEM] * 6,
+        in_specs=[VMEM] * 5,
         out_specs=VMEM,
         out_shape=table,
-        input_output_aliases={5: 0},
+        input_output_aliases={4: 0},
         compiler_params=params(8),
-        cost_estimate=cost(1312, 512),
-    )(own, up, down, beside, w1_v, ts)
+        cost_estimate=cost(1216, 512),
+    )(own, up, down, w1_v, ts)
 
     edge_out, node_out, _ = pl.pallas_call(
         layer_kernel,
-        in_specs=[SMEM] * 2 + [VMEM] * 17,
+        in_specs=[SMEM] * 2 + [VMEM] * 19,
         out_specs=[HBM, VMEM, VMEM],
         out_shape=[shape(4096, 512, bf16), shape(512, 512, bf16), table],
-        input_output_aliases={7: 2},
+        input_output_aliases={8: 2},
         scratch_shapes=[
             pltpu.VMEM((HALF * 4, 128), f32),
             pltpu.VMEM((HALF * 4, 128), f32),
@@ -376,9 +400,9 @@
         ],
         compiler_params=params(20),
     )(
-        place, bounds, recv_rows, part, edge_v, node_v, swapped, ts, w1_v,
+        place, bounds, recv_v, part, edge_v, node_v, swapped, beside, ts, w1_v,
         edge_w2, row(edge_b2), row(edge_gain), row(edge_shift),
-        node_part, node_w1, node_w2, row(node_b2), row(node_gain), row(node_shift),
+        node_part, node_w1, row(node_b1), node_w2, row(node_b2), row(node_gain), row(node_shift),
     )
     return edge_out, node_out
 

time: 60.1 us -> 57.7 us (0.960)
  the two profiles are of different devices: /device:TPU:1 before, /device:TPU:4 now
where the time goes in v1:
time: 57.7 us; the launch traced here: 57.5 us
  Pallas kernels  24.6 us (43%)
  starting transfers between devices  19.1 us (33%)
  waiting for transfers between devices  11.1 us (19%)
  local copies, waits for them, and re-layouts  1.58 us (3%)
  between operations  0.91 us (2%)
    pallas_call x1, Pallas kernels, on_device(): pl.pallas_call(layer_kernel, in_specs=[SMEM] * 2 + [VMEM] * 19, out_specs...  14.9 us
    ppermute x9, starting transfers between devices, ring_phase(): lax.ppermute(held, 'region', ring_route(phase, k))  13.3 us
    ppermute x1, waiting for transfers between devices, on_device(): lax.ppermute(jnp.where(core == 1, to_right, to_left), 'region', across)  6 us
    pallas_call x1, Pallas kernels, on_device(): pl.pallas_call(early_kernel, in_specs=[SMEM, VMEM, HBM] + [VMEM] * 4, out...  5.87 us
    ppermute x9, waiting for transfers between devices, ring_phase(): lax.ppermute(held, 'region', ring_route(phase, k))  5.11 us
    ppermute x2, starting transfers between devices, shifted(): lax.ppermute(jnp.concatenate(blocks, 0), 'region', linear_route(step))  4.27 us
    pallas_call x1, Pallas kernels, on_device(): pl.pallas_call(first_kernel, in_specs=[HBM] * 4 + [VMEM], out_specs=[VMEM...  2.97 us
    ppermute x1, starting transfers between devices, on_device(): lax.ppermute(jnp.where(core == 1, to_right, to_left), 'region', across)  1.39 us
  transfers between devices with their start and end apart: 13, of which 4 were waited for; matrix products, arithmetic and copies ran while one was open for 2% of the time, Pallas kernels for 17%

profile of v1, /device:TPU:4, one launch (start us, length us, event | category | flops | bytes accessed | tf_op | source)
XLA Modules:
  0.0 57.5 jit_solution(9573269709488489283)
XLA Ops:
  0.6 0.7 %slice.47 = bf16[16,512]{1,0:T(8,128)(2,1)S(1)} slice(bf16[512,512]{1,0:T(8,128)(2,1)} %node.1), slice={[0:16], [0:512]} | slice | bytes 32768 | tf_op jit(solution)/shard_map/slice | solution.py:319
  1.4 4.0 %collective-permute-start.2 = (bf16[16,512]{1,0:T(8,128)(2,1)S(1)}, bf16[16,512]{1,0:T(8,128)(2,1)S(1)}, u32[]{:S(2)}, u32[]{:S(2)}) collective-permute-start(bf16[16,512]{1,0:T(8,128)(2,1)S(1)} %slice.47), channel_id=1, source_target_pairs={{0,6},{1,97},{2,0},{3,99},{4,2},{5,101},{6,4},{7,103},{8,14},{9,10... | collective-permute-start | bytes 49160 | tf_op jit(solution)/shard_map/ppermute | solution.py:41
  5.4 0.0 collective-permute-start.1
  5.4 1.3 %collective-permute-start = (bf16[16,512]{1,0:T(8,128)(2,1)S(1)}, bf16[16,512]{1,0:T(8,128)(2,1)S(1)}, u32[]{:S(2)}, u32[]{:S(2)}) collective-permute-start(bf16[16,512]{1,0:T(8,128)(2,1)S(1)} %slice.47), channel_id=1, source_target_pairs={{0,2},{1,33},{2,4},{3,35},{4,6},{5,37},{6,0},{7,39},{8,10},{9,41},... | collective-permute-start | bytes 49160 | tf_op jit(solution)/shard_map/ppermute | solution.py:41
  6.6 0.8 %reshape.51.picks = s32[1,256]{1,0:T(1,128)S(1)} reshape(s32[1,8,32]{2,1,0:T(8,128)} %param.21) | data formatting | bytes 2048 | tf_op jit(solution)/shard_map/reshape | solution.py:311
  7.4 0.0 collective-permute-done.2
  7.4 3.2 %collective-permute-done.1 = bf16[16,512]{1,0:T(8,128)(2,1)S(1)} collective-permute-done((bf16[16,512]{1,0:T(8,128)(2,1)S(1)}, bf16[16,512]{1,0:T(8,128)(2,1)S(1)}, u32[]{:S(2)}, u32[]{:S(2)}) %collective-permute-start.1) | collective-permute-done | bytes 16416 | tf_op jit(solution)/shard_map/ppermute | solution.py:41
  10.6 0.0 collective-permute-done
  10.6 3.1 %collective-permute-start.5 = (bf16[64,512]{1,0:T(8,128)(2,1)S(1)}, bf16[64,512]{1,0:T(8,128)(2,1)S(1)}, u32[]{:S(2)}, u32[]{:S(2)}) collective-permute-start(bf16[64,512]{1,0:T(8,128)(2,1)S(1)} %pad_maximum_fusion.7), channel_id=1, source_target_pairs={{0,24},{1,7},{2,26},{3,1},{4,28},{5,3},{6,30},{7,5},{8,0},{9,15},{... | collective-permute-start | bytes 196616 | tf_op jit(solution)/shard_map/ppermute | solution.py:41
  13.7 0.6 %collective-permute-start.4 = (bf16[64,512]{1,0:T(8,128)(2,1)S(1)}, bf16[64,512]{1,0:T(8,128)(2,1)S(1)}, u32[]{:S(2)}, u32[]{:S(2)}) collective-permute-start(bf16[64,512]{1,0:T(8,128)(2,1)S(1)} %pad_maximum_fusion.7), channel_id=1, source_target_pairs={{0,16},{1,5},{2,18},{3,7},{4,20},{5,1},{6,22},{7,3},{8,24},{9,13},... | collective-permute-start | bytes 196616 | tf_op jit(solution)/shard_map/ppermute | solution.py:41
  14.4 1.0 %collective-permute-start.3 = (bf16[64,512]{1,0:T(8,128)(2,1)S(1)}, bf16[64,512]{1,0:T(8,128)(2,1)S(1)}, u32[]{:S(2)}, u32[]{:S(2)}) collective-permute-start(bf16[64,512]{1,0:T(8,128)(2,1)S(1)} %pad_maximum_fusion.7), channel_id=1, source_target_pairs={{0,8},{1,3},{2,10},{3,5},{4,12},{5,7},{6,14},{7,1},{8,16},{9,11},{... | collective-permute-start | bytes 196616 | tf_op jit(solution)/shard_map/ppermute | solution.py:41
  15.3 3.0 %shard_map.176 = (bf16[512,512]{1,0:T(8,128)(2,1)S(1)}, bf16[1536,512]{1,0:T(8,128)(2,1)S(1)}, s32[8,1,512]{2,1,0:T(1,128)S(1)}, bf16[640,512]{1,0:T(8,128)(2,1)...) custom-call(bf16[512,512]{1,0:T(8,128)(2,1)} %node.1, ...), custom_call_target="tpu_custom_call" | custom-call | flops 939524096 | bytes 5505024 | tf_op jit(solution)/shard_map/pallas_call | solution.py:322
  18.3 1.2 %collective-permute-done.4 = bf16[64,512]{1,0:T(8,128)(2,1)S(1)} collective-permute-done((bf16[64,512]{1,0:T(8,128)(2,1)S(1)}, bf16[64,512]{1,0:T(8,128)(2,1)S(1)}, u32[]{:S(2)}, u32[]{:S(2)}) %collective-permute-start.4) | collective-permute-done | bytes 65568 | tf_op jit(solution)/shard_map/ppermute | solution.py:41
  19.5 0.7 %collective-permute-done.3 = bf16[64,512]{1,0:T(8,128)(2,1)S(1)} collective-permute-done((bf16[64,512]{1,0:T(8,128)(2,1)S(1)}, bf16[64,512]{1,0:T(8,128)(2,1)S(1)}, u32[]{:S(2)}, u32[]{:S(2)}) %collective-permute-start.3) | collective-permute-done | bytes 65568 | tf_op jit(solution)/shard_map/ppermute | solution.py:41
  20.2 0.6 %collective-permute-start.8 = (bf16[256,512]{1,0:T(8,128)(2,1)S(1)}, bf16[256,512]{1,0:T(8,128)(2,1)S(1)}, u32[]{:S(2)}, u32[]{:S(2)}) collective-permute-start(bf16[256,512]{1,0:T(8,128)(2,1)S(1)} %pad_maximum_fusion.2), channel_id=1, source_target_pairs={{0,96},{1,25},{2,98},{3,27},{4,100},{5,29},{6,102},{7,31},{8,104},... | collective-permute-start | bytes 786440 | tf_op jit(solution)/shard_map/ppermute | solution.py:41
  20.8 2.7 %collective-permute-start.7 = (bf16[256,512]{1,0:T(8,128)(2,1)S(1)}, bf16[256,512]{1,0:T(8,128)(2,1)S(1)}, u32[]{:S(2)}, u32[]{:S(2)}) collective-permute-start(bf16[256,512]{1,0:T(8,128)(2,1)S(1)} %pad_maximum_fusion.2), channel_id=1, source_target_pairs={{0,64},{1,17},{2,66},{3,19},{4,68},{5,21},{6,70},{7,23},{8,72},{9,... | collective-permute-start | bytes 786440 | tf_op jit(solution)/shard_map/ppermute | solution.py:41
  23.7 0.1 collective-permute-start.9
  23.8 4.2 %collective-permute-start.10 = (bf16[96,512]{1,0:T(8,128)(2,1)S(1)}, bf16[96,512]{1,0:T(8,128)(2,1)S(1)}, u32[]{:S(2)}, u32[]{:S(2)}) collective-permute-start(bf16[96,512]{1,0:T(8,128)(2,1)S(1)} %pad_maximum_fusion.4), channel_id=1, source_target_pairs={{0,120},{1,121},{2,122},{3,123},{4,124},{5,125},{6,126},{7,127},{8... | collective-permute-start | bytes 294920 | tf_op jit(solution)/shard_map/ppermute | solution.py:46
  28.0 5.9 %shard_map.177 = (f32[4096,512]{1,0:T(8,128)S(1)}, bf16[4096,512]{1,0:T(8,128)(2,1)S(1)}) custom-call(s32[32]{0:T(128)S(1)} %get-tuple-element.34.bounds, s32[8,1,512]{2,1,0:T(1,128)S(1)} %get-tuple-element.35.recv_rows, bf16[4096,512]{1,0:T(8,128)(2,1)} %edge.1, bf16[1536,512]{1,0:T(8,128)(2,1)S(1)} %get-tuple-element.36.w1, f32[1,512]{1,0:T(1,128)S(1)} %bitcast.16, ...), custom_call_target="tpu_custom_call" | custom-call | flops 3221225472 | bytes 12582912 | tf_op jit(solution)/shard_map/pallas_call | solution.py:341
  33.9 0.1 pad_maximum_fusion.1.own
  34.0 0.1 pad_maximum_fusion
  34.1 0.1 collective-permute-start.11
  34.2 1.4 %collective-permute-start.12 = (bf16[96,512]{1,0:T(8,128)(2,1)S(1)}, bf16[96,512]{1,0:T(8,128)(2,1)S(1)}, u32[]{:S(2)}, u32[]{:S(2)}) collective-permute-start(bf16[96,512]{1,0:T(8,128)(2,1)S(1)} %get-tuple-element.60), channel_id=1, source_target_pairs={{0,127},{1,2},{2,1},{3,4},{4,3},{5,6},{6,5},{7,8},{8,7},{9,10},{10... | collective-permute-start | bytes 294920 | tf_op jit(solution)/shard_map/ppermute | solution.py:374
  35.6 0.0 copy-start.4
  35.6 0.0 copy-start.5
  35.6 0.0 copy-start.6
  35.6 0.0 copy-start.7
  35.6 0.0 copy-start.8
  35.7 0.0 copy-start.9
  35.7 0.9 %shard_map.178.old_ts = f32[11776,128]{1,0:T(8,128)S(1)} custom-call(bf16[1024,512]{1,0:T(8,128)(2,1)S(1)} %pad_maximum_fusion.1.own, bf16[96,512]{1,0:T(8,128)(2,1)S(1)} %collective-permute-done.9.up, bf16[96,512]{1,0:T(8,128)(2,1)S(1)} %collective-permute-done.10.down, bf16[1536,512]{1,0:T(8,128)(2,1)S(1)} %get-tuple-element.36.w1, ...), custom_call_target="tpu_custom_call", output_to_operand_aliasing={{}: (4, {})} | custom-call | flops 637534208 | bytes 3735552 | tf_op jit(solution)/shard_map/pallas_call | solution.py:375
  36.5 6.0 %collective-permute-done.12.beside = bf16[96,512]{1,0:T(8,128)(2,1)S(1)} collective-permute-done((bf16[96,512]{1,0:T(8,128)(2,1)S(1)}, bf16[96,512]{1,0:T(8,128)(2,1)S(1)}, u32[]{:S(2)}, u32[]{:S(2)}) %collective-permute-start.12) | collective-permute-done | bytes 98336 | tf_op jit(solution)/shard_map/ppermute | solution.py:374
  42.6 14.9 %shard_map.179 = (bf16[4096,512]{1,0:T(8,128)(2,1)}, bf16[512,512]{1,0:T(8,128)(2,1)}, f32[11776,128]{1,0:T(8,128)S(1)}) custom-call(s32[4608]{0:T(1024)S(1)} %pad.4.send_ref, s32[32]{0:T(128)S(1)} %get-tuple-element.34.bounds, s32[8,1,512]{2,1,0:T(1,128)S(1)} %get-tuple-element.35.recv_rows, ...), custom_call_target="tpu_custom_call", output_to_operand_aliasing={{2}: (8, {})} | custom-call | tf_op jit(solution)/shard_map/pallas_call | solution.py:385
  (35 shorter events, 0.2 us)
Async XLA Ops:
  1.4 6.1 %collective-permute-start.2 = (bf16[16,512]{1,0:T(8,128)(2,1)S(1)}, bf16[16,512]{1,0:T(8,128)(2,1)S(1)}, u32[]{:S(2)}, u32[]{:S(2)}) collective-permute-start(bf16[16,512]{1,0:T(8,128)(2,1)S(1)} %slice.47), channel_id=1, source_target_pairs={{0,6},{1,97},{2,0},{3,99},{4,2},{5,101},{6,4},{7,103},{8,14},{9,10... | collective-permute-start | bytes 49160 | tf_op jit(solution)/shard_map/ppermute | solution.py:41
  5.4 5.2 %collective-permute-start.1 = (bf16[16,512]{1,0:T(8,128)(2,1)S(1)}, bf16[16,512]{1,0:T(8,128)(2,1)S(1)}, u32[]{:S(2)}, u32[]{:S(2)}) collective-permute-start(bf16[16,512]{1,0:T(8,128)(2,1)S(1)} %slice.47), channel_id=1, source_target_pairs={{0,4},{1,65},{2,6},{3,67},{4,0},{5,69},{6,2},{7,71},{8,12},{9,73},... | collective-permute-start | bytes 49160 | tf_op jit(solution)/shard_map/ppermute | solution.py:41
  5.4 5.2 %collective-permute-start = (bf16[16,512]{1,0:T(8,128)(2,1)S(1)}, bf16[16,512]{1,0:T(8,128)(2,1)S(1)}, u32[]{:S(2)}, u32[]{:S(2)}) collective-permute-start(bf16[16,512]{1,0:T(8,128)(2,1)S(1)} %slice.47), channel_id=1, source_target_pairs={{0,2},{1,33},{2,4},{3,35},{4,6},{5,37},{6,0},{7,39},{8,10},{9,41},... | collective-permute-start | bytes 49160 | tf_op jit(solution)/shard_map/ppermute | solution.py:41
  10.6 7.7 %collective-permute-start.5 = (bf16[64,512]{1,0:T(8,128)(2,1)S(1)}, bf16[64,512]{1,0:T(8,128)(2,1)S(1)}, u32[]{:S(2)}, u32[]{:S(2)}) collective-permute-start(bf16[64,512]{1,0:T(8,128)(2,1)S(1)} %pad_maximum_fusion.7), channel_id=1, source_target_pairs={{0,24},{1,7},{2,26},{3,1},{4,28},{5,3},{6,30},{7,5},{8,0},{9,15},{... | collective-permute-start | bytes 196616 | tf_op jit(solution)/shard_map/ppermute | solution.py:41
  13.7 5.8 %collective-permute-start.4 = (bf16[64,512]{1,0:T(8,128)(2,1)S(1)}, bf16[64,512]{1,0:T(8,128)(2,1)S(1)}, u32[]{:S(2)}, u32[]{:S(2)}) collective-permute-start(bf16[64,512]{1,0:T(8,128)(2,1)S(1)} %pad_maximum_fusion.7), channel_id=1, source_target_pairs={{0,16},{1,5},{2,18},{3,7},{4,20},{5,1},{6,22},{7,3},{8,24},{9,13},... | collective-permute-start | bytes 196616 | tf_op jit(solution)/shard_map/ppermute | solution.py:41
  14.4 5.8 %collective-permute-start.3 = (bf16[64,512]{1,0:T(8,128)(2,1)S(1)}, bf16[64,512]{1,0:T(8,128)(2,1)S(1)}, u32[]{:S(2)}, u32[]{:S(2)}) collective-permute-start(bf16[64,512]{1,0:T(8,128)(2,1)S(1)} %pad_maximum_fusion.7), channel_id=1, source_target_pairs={{0,8},{1,3},{2,10},{3,5},{4,12},{5,7},{6,14},{7,1},{8,16},{9,11},{... | collective-permute-start | bytes 196616 | tf_op jit(solution)/shard_map/ppermute | solution.py:41
  15.3 8.3 %copy-start.11 = (s32[4096]{0:T(1024)S(1)}, s32[4096]{0:T(1024)}, u32[]{:S(2)}) copy-start(s32[4096]{0:T(1024)} %param.19) | copy-start | bytes 49156
  15.3 12.6 %copy-start.10 = (f32[512]{0:T(512)S(1)}, f32[512]{0:T(512)}, u32[]{:S(2)}) copy-start(f32[512]{0:T(512)} %param.23) | copy-start | bytes 6148
  20.2 13.6 %collective-permute-start.8 = (bf16[256,512]{1,0:T(8,128)(2,1)S(1)}, bf16[256,512]{1,0:T(8,128)(2,1)S(1)}, u32[]{:S(2)}, u32[]{:S(2)}) collective-permute-start(bf16[256,512]{1,0:T(8,128)(2,1)S(1)} %pad_maximum_fusion.2), channel_id=1, source_target_pairs={{0,96},{1,25},{2,98},{3,27},{4,100},{5,29},{6,102},{7,31},{8,104},... | collective-permute-start | bytes 786440 | tf_op jit(solution)/shard_map/ppermute | solution.py:41
  20.8 13.0 %collective-permute-start.7 = (bf16[256,512]{1,0:T(8,128)(2,1)S(1)}, bf16[256,512]{1,0:T(8,128)(2,1)S(1)}, u32[]{:S(2)}, u32[]{:S(2)}) collective-permute-start(bf16[256,512]{1,0:T(8,128)(2,1)S(1)} %pad_maximum_fusion.2), channel_id=1, source_target_pairs={{0,64},{1,17},{2,66},{3,19},{4,68},{5,21},{6,70},{7,23},{8,72},{9,... | collective-permute-start | bytes 786440 | tf_op jit(solution)/shard_map/ppermute | solution.py:41
  23.6 10.3 %collective-permute-start.6 = (bf16[256,512]{1,0:T(8,128)(2,1)S(1)}, bf16[256,512]{1,0:T(8,128)(2,1)S(1)}, u32[]{:S(2)}, u32[]{:S(2)}) collective-permute-start(bf16[256,512]{1,0:T(8,128)(2,1)S(1)} %pad_maximum_fusion.2), channel_id=1, source_target_pairs={{0,32},{1,9},{2,34},{3,11},{4,36},{5,13},{6,38},{7,15},{8,40},{9,1... | collective-permute-start | bytes 786440 | tf_op jit(solution)/shard_map/ppermute | solution.py:41
  23.7 10.3 %collective-permute-start.9 = (bf16[96,512]{1,0:T(8,128)(2,1)S(1)}, bf16[96,512]{1,0:T(8,128)(2,1)S(1)}, u32[]{:S(2)}, u32[]{:S(2)}) collective-permute-start(bf16[96,512]{1,0:T(8,128)(2,1)S(1)} %pad_maximum_fusion.3), channel_id=1, source_target_pairs={{0,8},{1,9},{2,10},{3,11},{4,12},{5,13},{6,14},{7,15},{8,16},{9,17... | collective-permute-start | bytes 294920 | tf_op jit(solution)/shard_map/ppermute | solution.py:46
  23.8 10.2 %collective-permute-start.10 = (bf16[96,512]{1,0:T(8,128)(2,1)S(1)}, bf16[96,512]{1,0:T(8,128)(2,1)S(1)}, u32[]{:S(2)}, u32[]{:S(2)}) collective-permute-start(bf16[96,512]{1,0:T(8,128)(2,1)S(1)} %pad_maximum_fusion.4), channel_id=1, source_target_pairs={{0,120},{1,121},{2,122},{3,123},{4,124},{5,125},{6,126},{7,127},{8... | collective-permute-start | bytes 294920 | tf_op jit(solution)/shard_map/ppermute | solution.py:46
  34.1 8.4 %collective-permute-start.11 = (bf16[1120,512]{1,0:T(8,128)(2,1)S(1)}, bf16[1120,512]{1,0:T(8,128)(2,1)S(1)}, u32[]{:S(2)}, u32[]{:S(2)}) collective-permute-start(bf16[1120,512]{1,0:T(8,128)(2,1)S(1)} %pad_maximum_fusion), channel_id=1, source_target_pairs={{0,1},{1,0},{2,3},{3,2},{4,5},{5,4},{6,7},{7,6},{8,9},{9,8},{10,11... | collective-permute-start | bytes 3440648 | tf_op jit(solution)/shard_map/ppermute | solution.py:370
  34.2 8.3 %collective-permute-start.12 = (bf16[96,512]{1,0:T(8,128)(2,1)S(1)}, bf16[96,512]{1,0:T(8,128)(2,1)S(1)}, u32[]{:S(2)}, u32[]{:S(2)}) collective-permute-start(bf16[96,512]{1,0:T(8,128)(2,1)S(1)} %get-tuple-element.60), channel_id=1, source_target_pairs={{0,127},{1,2},{2,1},{3,4},{4,3},{5,6},{6,5},{7,8},{8,7},{9,10},{10... | collective-permute-start | bytes 294920 | tf_op jit(solution)/shard_map/ppermute | solution.py:374
  35.6 7.0 %copy-start = (bf16[1024,512]{1,0:T(8,128)(2,1)S(1)}, bf16[1024,512]{1,0:T(8,128)(2,1)}, u32[]{:S(2)}) copy-start(bf16[1024,512]{1,0:T(8,128)(2,1)} %nw1.3) | copy-start | bytes 3145732
  35.6 7.0 %copy-start.1 = (bf16[512,512]{1,0:T(8,128)(2,1)S(1)}, bf16[512,512]{1,0:T(8,128)(2,1)}, u32[]{:S(2)}) copy-start(bf16[512,512]{1,0:T(8,128)(2,1)} %w2.1) | copy-start | bytes 1572868
  35.6 7.0 %copy-start.2 = (bf16[512,512]{1,0:T(8,128)(2,1)S(1)}, bf16[512,512]{1,0:T(8,128)(2,1)}, u32[]{:S(2)}) copy-start(bf16[512,512]{1,0:T(8,128)(2,1)} %nw2.1) | copy-start | bytes 1572868
  35.6 7.0 %copy-start.3 = (f32[512]{0:T(512)S(1)}, f32[512]{0:T(512)}, u32[]{:S(2)}) copy-start(f32[512]{0:T(512)} %param.25) | copy-start | bytes 6148
  35.6 7.0 %copy-start.4 = (f32[512]{0:T(512)S(1)}, f32[512]{0:T(512)}, u32[]{:S(2)}) copy-start(f32[512]{0:T(512)} %param.26) | copy-start | bytes 6148
  35.6 7.0 %copy-start.5 = (f32[512]{0:T(512)S(1)}, f32[512]{0:T(512)}, u32[]{:S(2)}) copy-start(f32[512]{0:T(512)} %param.27) | copy-start | bytes 6148
  35.6 7.0 %copy-start.6 = (f32[512]{0:T(512)S(1)}, f32[512]{0:T(512)}, u32[]{:S(2)}) copy-start(f32[512]{0:T(512)} %param.29) | copy-start | bytes 6148
  35.6 7.0 %copy-start.7 = (f32[512]{0:T(512)S(1)}, f32[512]{0:T(512)}, u32[]{:S(2)}) copy-start(f32[512]{0:T(512)} %param.31) | copy-start | bytes 6148
  35.6 7.0 %copy-start.8 = (f32[512]{0:T(512)S(1)}, f32[512]{0:T(512)}, u32[]{:S(2)}) copy-start(f32[512]{0:T(512)} %param.32) | copy-start | bytes 6148
  35.7 7.0 %copy-start.9 = (f32[512]{0:T(512)S(1)}, f32[512]{0:T(512)}, u32[]{:S(2)}) copy-start(f32[512]{0:T(512)} %param.33) | copy-start | bytes 6148
